TPU v7x, 32 devices: a whole 2x2x4 slice. The times are simulated.
32 devices in a mesh: dp: 8 (over z, core), chan: 4 (over y, x).
Axes of the slice: x: 2, y: 2, z: 4, core: 2. Of those that a mesh axis runs over, the one named last changes fastest.
Arguments:
- images: bfloat16 [16, 16, 16, 2816], P('dp', None, None, 'chan'), may hold values from -6 to 6
- kernel: float32 [7, 7, 2816], P(None, None, 'chan'), may hold values from -0.875 to 0.875
- layernorm_gain: float32 [2816], P('chan'), may hold values from 0.25 to 1.75
- layernorm_bias: float32 [2816], P('chan'), may hold values from -3 to 3
- w_expand: bfloat16 [2816, 11264], P('dp', 'chan'), may hold values from -0.109375 to 0.109375
- w_reduce: bfloat16 [11264, 2816], P('chan', 'dp'), may hold values from -0.0546875 to 0.0546875
- layer_scale: float32 [2816], P('chan'), may hold values from 0.25 to 1
- cotangent: bfloat16 [16, 16, 16, 2816], P('dp', None, None, 'chan'), may hold values from -6 to 6
Outputs:
- output: bfloat16 [16, 16, 16, 2816], P('dp', None, None, 'chan')
- grad_images: bfloat16 [16, 16, 16, 2816], P('dp', None, None, 'chan')
- grad_kernel: float32 [7, 7, 2816], P(None, None, 'chan')
- gain_gradient: float32 [2816], P('chan')
- grad_bias: float32 [2816], P('chan')
- grad_expand: float32 [2816, 11264], P('dp', 'chan')
- grad_reduce: float32 [11264, 2816], P('chan', 'dp')
- grad_scale: float32 [2816], P('chan')
All inputs are finite; a program needn't handle non-finite values.
Results may differ from a plain program's by a relative error of at most 0.025.
Values may be sent and summed in bfloat16 or wider, within the bound.
A program may use at most 128 MiB of HBM per device.

v0:
```python
import math
import jax
import jax.numpy as jnp
from jax import lax
from jax.sharding import PartitionSpec as P

eps = 1e-06


def depthwise(field, kern):
    height = field.shape[1]
    breadth = field.shape[2]
    padded = jnp.pad(field, ((0, 0), (3, 3), (3, 3), (0, 0)))
    total = jnp.zeros(field.shape, jnp.float32)
    for i in range(7):
        for j in range(7):
            total = total + padded[:, i : i + height, j : j + breadth, :] * kern[i, j]
    return total


def normal_cdf(value):
    return 0.5 * (1.0 + jax.scipy.special.erf(value / math.sqrt(2.0)))


def body(
    images, kernel, layernorm_gain, layernorm_bias, w_expand, w_reduce, layer_scale, cotangent
):
    shape_in = images.shape
    height = shape_in[1]
    breadth = shape_in[2]
    positions = shape_in[0] * height * breadth
    local_chan = shape_in[3]
    image_width = local_chan * lax.axis_size("chan")
    xf = images.astype(jnp.float32)
    conv = depthwise(xf, kernel).reshape(positions, local_chan)
    mean_val = lax.psum(jnp.sum(conv, axis=1), "chan")[:, None] / image_width
    centred_rows = conv - mean_val
    var = lax.psum(jnp.sum(centred_rows * centred_rows, axis=1), "chan")[:, None] / image_width
    inverse_deviation = lax.rsqrt(var + eps)
    standardized_input = centred_rows * inverse_deviation
    normed_output = (standardized_input * layernorm_gain + layernorm_bias).astype(jnp.bfloat16)
    normed_all = lax.all_gather(normed_output, "chan", axis=1, tiled=True)
    expand_all = lax.all_gather(w_expand, "dp", axis=0, tiled=True)
    pre = jnp.dot(normed_all, expand_all, preferred_element_type=jnp.float32)
    hidden = (pre * normal_cdf(pre)).astype(jnp.bfloat16)
    reduce_all = lax.all_gather(w_reduce, "dp", axis=1, tiled=True)
    partial_branch = jnp.dot(hidden, reduce_all, preferred_element_type=jnp.float32)
    branch = lax.psum_scatter(
        partial_branch.astype(jnp.bfloat16), "chan", scatter_dimension=1, tiled=True
    ).astype(jnp.float32)
    xr = xf.reshape(positions, local_chan)
    output = (xr + layer_scale * branch).astype(jnp.bfloat16).reshape(shape_in)
    dyf = cotangent.astype(jnp.float32).reshape(positions, local_chan)
    scale_part = jnp.sum(dyf * branch, axis=0)
    dbranch = (dyf * layer_scale).astype(jnp.bfloat16)
    dbranch_all = lax.all_gather(dbranch, "chan", axis=1, tiled=True)
    dhidden = lax.dot_general(
        dbranch_all, reduce_all, (((1,), (1,)), ((), ())), preferred_element_type=jnp.float32
    )
    slope = normal_cdf(pre) + pre * jnp.exp(-0.5 * pre * pre) / math.sqrt(2.0 * math.pi)
    dpre = (dhidden * slope).astype(jnp.bfloat16)
    columns = normed_all
    grad_expand = lax.psum_scatter(
        lax.dot_general(
            columns, dpre, (((0,), (0,)), ((), ())), preferred_element_type=jnp.float32
        ).astype(jnp.bfloat16),
        "dp",
        scatter_dimension=0,
        tiled=True,
    ).astype(jnp.float32)
    partial_normed = lax.dot_general(
        dpre, expand_all, (((1,), (1,)), ((), ())), preferred_element_type=jnp.float32
    )
    normed_grad = lax.psum_scatter(
        partial_normed.astype(jnp.bfloat16), "chan", scatter_dimension=1, tiled=True
    ).astype(jnp.float32)
    columns = dbranch_all
    grad_reduce = (
        lax.psum_scatter(
            lax.dot_general(
                columns, hidden, (((0,), (0,)), ((), ())), preferred_element_type=jnp.float32
            ).astype(jnp.bfloat16),
            "dp",
            scatter_dimension=0,
            tiled=True,
        )
        .astype(jnp.float32)
        .T
    )
    gain_partial = jnp.sum(normed_grad * standardized_input, axis=0)
    bias_part = jnp.sum(normed_grad, axis=0)
    standardized_grad = normed_grad * layernorm_gain
    first_half, second_half = lax.psum(
        (
            jnp.sum(standardized_grad, axis=1),
            jnp.sum(standardized_grad * standardized_input, axis=1),
        ),
        "chan",
    )
    conv_output_grad = inverse_deviation * (
        standardized_grad
        - first_half[:, None] / image_width
        - standardized_input * (second_half[:, None] / image_width)
    )
    conv_output_grad = conv_output_grad.reshape(shape_in)
    padded = jnp.pad(xf, ((0, 0), (3, 3), (3, 3), (0, 0)))
    dpad = jnp.pad(conv_output_grad, ((0, 0), (3, 3), (3, 3), (0, 0)))
    back = cotangent.astype(jnp.float32)
    kern_rows = []
    for i in range(7):
        tap_row = []
        for j in range(7):
            tap_row.append(
                jnp.sum(
                    padded[:, i : i + height, j : j + breadth, :] * conv_output_grad, axis=(0, 1, 2)
                )
            )
            back = back + dpad[:, 6 - i : 6 - i + height, 6 - j : 6 - j + breadth, :] * kernel[i, j]
        kern_rows.append(jnp.stack(tap_row))
    kernel_part = jnp.stack(kern_rows)
    grad_images = back.astype(jnp.bfloat16)
    grad_kernel, gain_gradient, grad_bias, grad_scale = (
        lax.psum(kernel_part.astype(jnp.bfloat16), "dp").astype(jnp.float32),
        lax.psum(gain_partial.astype(jnp.bfloat16), "dp").astype(jnp.float32),
        lax.psum(bias_part.astype(jnp.bfloat16), "dp").astype(jnp.float32),
        lax.psum(scale_part.astype(jnp.bfloat16), "dp").astype(jnp.float32),
    )
    return (
        output,
        grad_images,
        grad_kernel,
        gain_gradient,
        grad_bias,
        grad_expand,
        grad_reduce,
        grad_scale,
    )


def solution(mesh):
    in_specs = (
        P("dp", None, None, "chan"),
        P(None, None, "chan"),
        P("chan"),
        P("chan"),
        P("dp", "chan"),
        P("chan", "dp"),
        P("chan"),
        P("dp", None, None, "chan"),
    )
    out_specs = (
        P("dp", None, None, "chan"),
        P("dp", None, None, "chan"),
        P(None, None, "chan"),
        P("chan"),
        P("chan"),
        P("dp", "chan"),
        P("chan", "dp"),
        P("chan"),
    )
    return jax.shard_map(body, mesh=mesh, in_specs=in_specs, out_specs=out_specs, check_vma=False)
```

profile of v0, /device:TPU:0, one launch (start us, length us, event | category | flops | bytes accessed | tf_op | source)
XLA Modules:
  0.0 969.2 jit_solution(17701858807250672959)
XLA Ops:
  7.2 0.0 all-gather.5.cloned.1.call-start
  7.2 1.2 slice_reduce_fusion.46
  8.4 1.4 slice_reduce_fusion.48
  9.7 1.4 slice_reduce_fusion.47
  11.2 1.3 convert_element_type.71
  12.5 12.3 %fusion.114 = (f32[2,16,16]{2,1,0:T(8,128)S(1)}, f32[2,16,16,704]{3,2,1,0:T(8,128)S(1)}) fusion(f32[704]{0:T(1024)S(1)} %get-tuple-element.115, f32[704]{0:T(1024)S(1)} %get-tuple-element.116, f32[704]{0:T(1024)S(1)} %get-tuple-element.69, f32[704]{0:T(1024)S(1)} %get-tuple-element.70, f32[704]{0:T(1024)S(1)} %get-tuple-element.71, ...), kind=kLoop, calls=%fused_computation.336 | loop fusion | flops 35323392 | bytes 3023616 | tf_op jit(solution)/shard_map/reduce_sum | solution.py:36
  24.8 0.1 reduce_sum.512
  24.9 11.3 %psum.56 = f32[512]{0:T(512)S(1)} all-reduce(f32[512]{0:T(512)S(1)} %reduce_sum.512), channel_id=1, replica_groups=mesh['dp'=8,'chan'=4] {'chan'}, use_global_device_ids=true, to_apply=%region_1.2 | all-reduce | flops 512 | bytes 4096 | tf_op jit(solution)/shard_map/psum | solution.py:36
  36.2 0.1 sub.28
  36.3 0.3 multiply_reduce_fusion.49
  36.7 0.1 reduce_sum.514
  36.7 8.0 psum.57
  44.7 1.9 copy.71
  46.6 1.1 add_convert_fusion
  47.7 0.0 all-gather.5.cloned.1.call-update
  47.7 0.0 all-gather.7.cloned.1.call-start
  47.8 0.7 all-gather.7.cloned.1.call-update
  48.5 0.0 all-gather.9.cloned.1.call-start
  48.5 0.7 all-gather.9.cloned.1.call-update
  49.2 0.3 reduce-scatter.5.cloned.1.call-start
  49.6 40.4 %all-gather.5.cloned.1.call-done = bf16[512,2816]{0,1:T(8,128)(2,1)} async-done(((bf16[512,704]{0,1:T(8,128)(2,1)}), bf16[512,2816]{0,1:T(8,128)(2,1)}) %all-gather.5.cloned.1.call-update) | async-done | bytes 2883600 | tf_op jit(solution)/shard_map/all_gather | solution.py:42
  90.0 145.3 %all-gather.7.cloned.1.call-done = bf16[2816,2816]{1,0:T(8,128)(2,1)} async-done(((bf16[352,2816]{1,0:T(8,128)(2,1)}), bf16[2816,2816]{1,0:T(8,128)(2,1)}) %all-gather.7.cloned.1.call-update) | async-done | bytes 15859728 | tf_op jit(solution)/shard_map/all_gather | solution.py:43
  235.3 15.1 %fusion.115 = f32[512,2816]{1,0:T(8,128)} fusion(bf16[512,2816]{0,1:T(8,128)(2,1)} %all-gather.5.cloned.1.call-done, bf16[2816,2816]{1,0:T(8,128)(2,1)} %all-gather.7.cloned.1.call-done), kind=kOutput, calls=%fused_computation.337 | convolution fusion | flops 8120172544 | bytes 24510464 | tf_op jit(solution)/shard_map/dot_general | solution.py:44
  250.3 128.5 %all-gather.9.cloned.1.call-done = bf16[2816,2816]{0,1:T(8,128)(2,1)} async-done(((bf16[2816,352]{0,1:T(8,128)(2,1)}), bf16[2816,2816]{0,1:T(8,128)(2,1)}) %all-gather.9.cloned.1.call-update) | async-done | bytes 15859728 | tf_op jit(solution)/shard_map/all_gather | solution.py:46
  378.8 16.3 %convolution_convert_fusion.3 = bf16[512,2816]{0,1:T(8,128)(2,1)} fusion(bf16[2816,2816]{0,1:T(8,128)(2,1)} %all-gather.9.cloned.1.call-done, f32[512,2816]{1,0:T(8,128)} %fusion.115), kind=kOutput, calls=%fused_computation.108 | convolution fusion | flops 8128823296 | bytes 24510464 | tf_op jit(solution)/shard_map/dot_general | solution.py:47
  395.1 0.0 reduce-scatter.5.cloned.1.call-update
  395.1 0.0 all-gather.11.cloned.1.call-start
  395.1 2.5 copy.74
  397.6 1.6 copy.72
  399.3 36.0 %reduce-scatter.5.cloned.1.call-done = bf16[512,704]{0,1:T(8,128)(2,1)} async-done(((bf16[512,2816]{0,1:T(8,128)(2,1)}), bf16[512,704]{0,1:T(8,128)(2,1)}) %reduce-scatter.5.cloned.1.call-update) | async-done | bytes 720912 | tf_op jit(solution)/shard_map/reduce_scatter | solution.py:48
  435.3 3.5 fusion.109
  438.8 0.6 reduce-scatter.7.cloned.1.call-start
  439.4 41.4 %all-gather.11.cloned.1.call-done = bf16[512,2816]{0,1:T(8,128)(2,1)} async-done(((bf16[512,704]{0,1:T(8,128)(2,1)}), bf16[512,2816]{0,1:T(8,128)(2,1)}) %all-gather.11.cloned.1.call-update) | async-done | bytes 2883600 | tf_op jit(solution)/shard_map/all_gather | solution.py:56
  480.7 16.0 %fusion.5 = bf16[512,2816]{1,0:T(8,128)(2,1)S(1)} fusion(f32[512,2816]{1,0:T(8,128)} %fusion.115, bf16[512,2816]{0,1:T(8,128)(2,1)} %all-gather.11.cloned.1.call-done, bf16[2816,2816]{0,1:T(8,128)(2,1)} %all-gather.9.cloned.1.call-done), kind=kOutput, calls=%fused_computation.104 | convolution fusion | flops 8134590464 | bytes 27394048 | tf_op jit(solution)/shard_map/dot_general | solution.py:57
  496.8 1.6 copy-done.7
  498.3 13.0 %convolution_convert_fusion.2 = bf16[512,2816]{0,1:T(8,128)(2,1)} fusion(bf16[512,2816]{1,0:T(8,128)(2,1)S(1)} %fusion.5, bf16[2816,2816]{1,0:T(8,128)(2,1)} %all-gather.7.cloned.1.call-done), kind=kOutput, calls=%fused_computation.107 | convolution fusion | flops 8121614336 | bytes 21626880 | tf_op jit(solution)/shard_map/dot_general | solution.py:71
  511.4 0.0 all-reduce.6.cloned.1.call-start
  511.4 41.9 %reduce-scatter.7.cloned.1.call-done = bf16[512,704]{0,1:T(8,128)(2,1)} async-done(((bf16[512,2816]{0,1:T(8,128)(2,1)}), bf16[512,704]{0,1:T(8,128)(2,1)}) %reduce-scatter.7.cloned.1.call-update) | async-done | bytes 720912 | tf_op jit(solution)/shard_map/reduce_scatter | solution.py:74
  553.3 1.7 fusion.113
  555.0 9.1 all-reduce.2
  564.1 2.6 fusion.111
  566.8 1.8 copy.75
  568.6 3.8 multiply_reduce_fusion.2
  572.4 4.2 multiply_reduce_fusion
  576.7 4.5 multiply_reduce_fusion.1
  582.2 0.6 copy-done.3
  582.8 0.0 all-reduce.6.cloned.1.call-update
  582.9 0.0 reduce-scatter.11.cloned.1.call-start
  582.9 15.4 %convolution_convert_fusion = bf16[2816,2816]{1,0:T(8,128)(2,1)} fusion(bf16[512,2816]{0,1:T(8,128)(2,1)} %all-gather.11.cloned.1.call-done, f32[512,2816]{1,0:T(8,128)} %fusion.115), kind=kOutput, calls=%fused_computation.96 | convolution fusion | flops 8135311360 | bytes 24510464 | tf_op jit(solution)/shard_map/dot_general | solution.py:80
  598.4 0.3 reduce-scatter.9.cloned.1.call-start
  598.6 13.9 %convolution_convert_fusion.1 = bf16[2816,2816]{1,0:T(8,128)(2,1)} fusion(bf16[512,2816]{0,1:T(8,128)(2,1)} %all-gather.5.cloned.1.call-done, bf16[512,2816]{1,0:T(8,128)(2,1)} %copy-done.7), kind=kOutput, calls=%fused_computation.97 | convolution fusion | flops 8128102400 | bytes 21626880 | tf_op jit(solution)/shard_map/dot_general | solution.py:64
  612.5 0.0 reduce-scatter.9.cloned.1.call-update
  612.6 2.4 copy.73
  615.0 0.2 reduce_sum.567
  615.2 14.6 %all-reduce.3 = (bf16[704]{0:T(1024)(128)(2,1)S(1)}, bf16[704]{0:T(1024)(128)(2,1)S(1)}, bf16[704]{0:T(1024)(128)(2,1)S(1)}) all-reduce(bf16[704]{0:T(1024)(128)(2,1)S(1)} %get-tuple-element.64, bf16[704]{0:T(1024)(128)(2,1)S(1)} %reduce_sum.567, bf16[704]{0:T(1024)(128)(2,1)S(1)} %get-tuple-element.124), channel_id=1, replica_groups=mesh['dp'=8,'chan'=4] {'dp'}, use_global_device_ids=true, to_apply=%region_61.62 | all-reduce | flops 2112 | bytes 8448 | tf_op jit(solution)/shard_map/psum | solution.py:124
  629.8 0.6 convert_element_type.85
  630.4 0.6 convert_element_type.86
  631.0 0.6 convert_element_type.91
  631.6 12.3 %fusion.102 = bf16[2,16,16,704]{3,2,1,0:T(8,128)(2,1)} fusion(f32[2,16,16,704]{3,2,1,0:T(8,128)S(1)} %bitcast.82, f32[704]{0:T(1024)S(1)} %get-tuple-element.115, f32[704]{0:T(1024)S(1)} %get-tuple-element.116, f32[704]{0:T(1024)S(1)} %get-tuple-element.69, f32[704]{0:T(1024)S(1)} %get-tuple-element.70, f32[704]{0:T(1024)S(1)} %get-tuple-element.71, ...), kind=kLoop, calls=%fused_computation.210 | loop fusion | flops 36044800 | bytes 3021568 | tf_op jit(solution)/shard_map/convert_element_type | solution.py:121
  643.9 1.6 convert_element_type.83
  645.5 152.7 %reduce-scatter.11.cloned.1.call-done = bf16[352,2816]{1,0:T(8,128)(2,1)} async-done(((bf16[2816,2816]{1,0:T(8,128)(2,1)}), bf16[352,2816]{1,0:T(8,128)(2,1)}) %reduce-scatter.11.cloned.1.call-update) | async-done | bytes 1982480 | tf_op jit(solution)/shard_map/reduce_scatter | solution.py:79
  798.2 3.7 convert_bitcast_fusion
  801.9 156.8 %reduce-scatter.9.cloned.1.call-done = bf16[352,2816]{1,0:T(8,128)(2,1)} async-done(((bf16[2816,2816]{1,0:T(8,128)(2,1)}), bf16[352,2816]{1,0:T(8,128)(2,1)}) %reduce-scatter.9.cloned.1.call-update) | async-done | bytes 1982480 | tf_op jit(solution)/shard_map/reduce_scatter | solution.py:63
  958.7 3.7 convert_element_type.88
  (84 shorter events, 0.7 us)
Async XLA Ops:
  7.2 82.8 %all-gather.5.cloned.1.call-start = ((), (), s32[]{:S(2)}) async-start(), calls=%async_computation.4 | async-start | bytes 3604480 | tf_op jit(solution)/shard_map/all_gather | solution.py:42
  24.8 19.9 %copy-start = (f32[2,16,16,704]{3,2,1,0:T(8,128)}, f32[2,16,16,704]{3,2,1,0:T(8,128)S(1)}, u32[]{:S(2)}) copy-start(f32[2,16,16,704]{3,2,1,0:T(8,128)S(1)} %get-tuple-element.123) | copy-start | bytes 4325380
  36.6 9.9 %copy-start.4 = (f32[704]{0:T(1024)S(1)}, f32[704]{0:T(1024)}, u32[]{:S(2)}) copy-start(f32[704]{0:T(1024)} %param.10) | copy-start | bytes 8452
  36.6 9.9 %copy-start.5 = (f32[704]{0:T(1024)S(1)}, f32[704]{0:T(1024)}, u32[]{:S(2)}) copy-start(f32[704]{0:T(1024)} %param.11) | copy-start | bytes 8452
  47.7 187.5 %all-gather.7.cloned.1.call-start = ((), (), s32[]{:S(2)}) async-start(), calls=%async_computation.5 | async-start | bytes 17842176 | tf_op jit(solution)/shard_map/all_gather | solution.py:43
  48.5 330.3 %all-gather.9.cloned.1.call-start = ((), (), s32[]{:S(2)}) async-start(), calls=%async_computation.6 | async-start | bytes 17842176 | tf_op jit(solution)/shard_map/all_gather | solution.py:46
  49.2 386.0 %reduce-scatter.5.cloned.1.call-start = ((), (), s32[]{:S(2)}) async-start(), calls=%async_computation.7 | async-start | bytes 3604480 | tf_op jit(solution)/shard_map/reduce_scatter | solution.py:48
  395.1 85.6 %all-gather.11.cloned.1.call-start = ((), (), s32[]{:S(2)}) async-start(), calls=%async_computation.8 | async-start | bytes 3604480 | tf_op jit(solution)/shard_map/all_gather | solution.py:56
  397.6 37.6 %copy-start.6 = (f32[704]{0:T(1024)S(1)}, f32[704]{0:T(1024)}, u32[]{:S(2)}) copy-start(f32[704]{0:T(1024)} %param.14) | copy-start | bytes 8452
  438.8 114.5 %reduce-scatter.7.cloned.1.call-start = ((), (), s32[]{:S(2)}) async-start(), calls=%async_computation.9 | async-start | bytes 3604480 | tf_op jit(solution)/shard_map/reduce_scatter | solution.py:74
  496.8 1.6 copy-start.7
  511.4 132.5 %all-reduce.6.cloned.1.call-start = ((), (), s32[]{:S(2)}) async-start(), calls=%async_computation.10 | async-start | bytes 172032 | tf_op jit(solution)/shard_map/psum | solution.py:123
  582.2 0.6 copy-start.3
  582.9 215.3 %reduce-scatter.11.cloned.1.call-start = ((), (), s32[]{:S(2)}) async-start(), calls=%async_computation.12 | async-start | bytes 17842176 | tf_op jit(solution)/shard_map/reduce_scatter | solution.py:79
  598.4 360.3 %reduce-scatter.9.cloned.1.call-start = ((), (), s32[]{:S(2)}) async-start(), calls=%async_computation.11 | async-start | bytes 17842176 | tf_op jit(solution)/shard_map/reduce_scatter | solution.py:63
  612.6 2.4 copy-start.1
  612.6 19.0 %copy-start.2 = (bf16[2,16,16,704]{3,2,1,0:T(8,128)(2,1)S(1)}, bf16[2,16,16,704]{3,2,1,0:T(8,128)(2,1)}, u32[]{:S(2)}) copy-start(bf16[2,16,16,704]{3,2,1,0:T(8,128)(2,1)} %param.15) | copy-start | bytes 2162692
Sparse Core Ops, SparseCore 0:
  47.9 42.1 all-gather.4
  91.7 143.5 all-gather.6
  236.9 141.8 all-gather.8
  395.2 39.9 reduce-scatter.4
  438.9 41.7 all-gather.10
  511.5 41.7 reduce-scatter.6
  583.0 49.9 all-reduce.5
  635.5 162.6 reduce-scatter.10
  800.7 157.9 reduce-scatter.8
where the time goes:
time: 974 us; the launch traced here: 969 us
  waiting for transfers between devices  744 us (76%)
  matrix products  89.7 us (9%)
  other arithmetic  58.8 us (6%)
  blocking collectives  43 us (4%)
  local copies, waits for them, and re-layouts  17.3 us (2%)
  between operations  14.7 us (2%)
    reduce_scatter x1, waiting for transfers between devices, body(): lax.psum_scatter(lax.dot_general(columns, dpre, (((0,), (0,)), ((), ())),...  157 us
    reduce_scatter x1, waiting for transfers between devices, body(): lax.psum_scatter(lax.dot_general(columns, hidden, (((0,), (0,)), ((), ())...  153 us
    all_gather x1, waiting for transfers between devices, body(): expand_all = lax.all_gather(w_expand, 'dp', axis=0, tiled=True)  145 us
    all_gather x1, waiting for transfers between devices, body(): reduce_all = lax.all_gather(w_reduce, 'dp', axis=1, tiled=True)  128 us
    reduce_scatter x1, waiting for transfers between devices, body(): lax.psum_scatter(partial_normed.astype(jnp.bfloat16), 'chan', scatter_dim...  41.9 us
    all_gather x1, waiting for transfers between devices, body(): dbranch_all = lax.all_gather(dbranch, 'chan', axis=1, tiled=True)  41.4 us
    all_gather x1, waiting for transfers between devices, body(): normed_all = lax.all_gather(normed_output, 'chan', axis=1, tiled=True)  40.4 us
    reduce_scatter x1, waiting for transfers between devices, body(): lax.psum_scatter(partial_branch.astype(jnp.bfloat16), 'chan', scatter_dim...  36 us
  transfers between devices with their start and end apart: 9, of which 8 were waited for; matrix products, arithmetic and copies ran while one was open for 7% of the time, Pallas kernels for 0%

commit v1 on v0

--- a/solution.py
+++ b/solution.py
@@ -5,6 +5,18 @@
 from jax.sharding import PartitionSpec as P
 
 eps = 1e-06
+
+
+def collect(shard, axis, dim):
+    ways, here = (lax.axis_size(axis), lax.axis_index(axis))
+    grown, reach = (shard, 1)
+    while reach < ways:
+        theirs = lax.ppermute(grown, axis, [(d, d ^ reach) for d in range(ways)])
+        mine_first = jnp.concatenate([grown, theirs], axis=dim)
+        theirs_first = jnp.concatenate([theirs, grown], axis=dim)
+        grown = jnp.where(here & reach == 0, mine_first, theirs_first)
+        reach = 2 * reach
+    return grown
 
 
 def depthwise(field, kern):
@@ -39,7 +51,7 @@
     inverse_deviation = lax.rsqrt(var + eps)
     standardized_input = centred_rows * inverse_deviation
     normed_output = (standardized_input * layernorm_gain + layernorm_bias).astype(jnp.bfloat16)
-    normed_all = lax.all_gather(normed_output, "chan", axis=1, tiled=True)
+    normed_all = collect(normed_output, "chan", 1)
     expand_all = lax.all_gather(w_expand, "dp", axis=0, tiled=True)
     pre = jnp.dot(normed_all, expand_all, preferred_element_type=jnp.float32)
     hidden = (pre * normal_cdf(pre)).astype(jnp.bfloat16)

time: 974 us -> 894 us (0.918)
  waiting for transfers between devices: 744 us -> 660 us
    all_gather x1, waiting for transfers between devices: 145 us -> 61 us  [body(): expand_all = lax.all_gather(w_expand, 'dp', axis=0, tiled=True)]
    ppermute x0 -> x2, waiting for transfers between devices: none -> 44 us  [collect(): theirs = lax.ppermute(grown, axis, [(d, d ^ reach) for d in range(ways)])]
    all_gather x1 -> x0, waiting for transfers between devices: 40.4 us -> none  [body(): normed_all = lax.all_gather(normed_output, 'chan', axis=1, tiled=True)]
  transfers between devices with their start and end apart: 9 -> 10, of which waited for: 8 -> 9; matrix products, arithmetic and copies ran while one was open for 7% -> 11% of each run, Pallas kernels for 0% -> 0%
where the time goes in v1:
time: 894 us; the launch traced here: 890 us
  waiting for transfers between devices  660 us (74%)
  matrix products  93.7 us (10%)
  other arithmetic  61 us (7%)
  blocking collectives  43.3 us (5%)
  between operations  15 us (2%)
  local copies, waits for them, and re-layouts  14.4 us (2%)
    reduce_scatter x1, waiting for transfers between devices, body(): lax.psum_scatter(lax.dot_general(columns, dpre, (((0,), (0,)), ((), ())),...  157 us
    reduce_scatter x1, waiting for transfers between devices, body(): lax.psum_scatter(lax.dot_general(columns, hidden, (((0,), (0,)), ((), ())...  150 us
    all_gather x1, waiting for transfers between devices, body(): reduce_all = lax.all_gather(w_reduce, 'dp', axis=1, tiled=True)  127 us
    all_gather x1, waiting for transfers between devices, body(): expand_all = lax.all_gather(w_expand, 'dp', axis=0, tiled=True)  61 us
    ppermute x2, waiting for transfers between devices, collect(): theirs = lax.ppermute(grown, axis, [(d, d ^ reach) for d in range(ways)])  44 us
    reduce_scatter x1, waiting for transfers between devices, body(): lax.psum_scatter(partial_normed.astype(jnp.bfloat16), 'chan', scatter_dim...  41.9 us
    all_gather x1, waiting for transfers between devices, body(): dbranch_all = lax.all_gather(dbranch, 'chan', axis=1, tiled=True)  41.4 us
    reduce_scatter x1, waiting for transfers between devices, body(): lax.psum_scatter(partial_branch.astype(jnp.bfloat16), 'chan', scatter_dim...  36 us
  transfers between devices with their start and end apart: 10, of which 9 were waited for; matrix products, arithmetic and copies ran while one was open for 11% of the time, Pallas kernels for 0%

profile of v1, /device:TPU:0, one launch (start us, length us, event | category | flops | bytes accessed | tf_op | source)
XLA Modules:
  0.0 890.2 jit_solution(1510450923336707750)
XLA Ops:
  7.2 0.0 all-gather.4.cloned.1.call-start
  7.2 0.7 all-gather.4.cloned.1.call-update
  7.9 0.0 all-gather.6.cloned.1.call-start
  8.0 0.7 all-gather.6.cloned.1.call-update
  8.7 0.0 reduce-scatter.5.cloned.1.call-start
  8.7 0.2 convert_element_type.71
  8.9 0.7 copy-done.4
  9.6 0.1 slice_reduce_fusion.46
  9.7 0.2 slice_reduce_fusion.48
  9.8 0.2 slice_reduce_fusion.47
  10.0 12.3 %fusion.117 = (f32[2,16,16]{2,1,0:T(8,128)S(1)}, f32[2,16,16,704]{3,2,1,0:T(8,128)S(1)}) fusion(f32[704]{0:T(1024)S(1)} %get-tuple-element.115, f32[704]{0:T(1024)S(1)} %get-tuple-element.116, f32[704]{0:T(1024)S(1)} %get-tuple-element.69, f32[704]{0:T(1024)S(1)} %get-tuple-element.70, f32[704]{0:T(1024)S(1)} %get-tuple-element.71, ...), kind=kLoop, calls=%fused_computation.341 | loop fusion | flops 35323392 | bytes 3023616 | tf_op jit(solution)/shard_map/reduce_sum | solution.py:48
  22.3 0.1 reduce_sum.512
  22.4 11.3 %psum.56 = f32[512]{0:T(512)S(1)} all-reduce(f32[512]{0:T(512)S(1)} %reduce_sum.512), channel_id=1, replica_groups=mesh['dp'=8,'chan'=4] {'chan'}, use_global_device_ids=true, to_apply=%region_1.2 | all-reduce | flops 512 | bytes 4096 | tf_op jit(solution)/shard_map/psum | solution.py:48
  33.8 0.1 sub.28
  33.9 0.3 multiply_reduce_fusion.49
  34.2 0.1 reduce_sum.514
  34.3 1.9 copy.71
  36.1 8.3 psum.57
  44.4 1.1 add_convert_fusion
  45.6 1.5 collective-permute-start
  47.0 14.3 %collective-permute-done = bf16[512,704]{0,1:T(8,128)(2,1)} collective-permute-done((bf16[512,704]{0,1:T(8,128)(2,1)}, bf16[512,704]{0,1:T(8,128)(2,1)}, u32[]{:S(2)}, u32[]{:S(2)}) %collective-permute-start) | collective-permute-done | bytes 720928 | tf_op jit(solution)/shard_map/ppermute | solution.py:14
  61.3 3.4 maximum_select_fusion.1
  64.7 0.6 collective-permute-start.1
  65.3 29.7 %collective-permute-done.1 = bf16[512,1408]{0,1:T(8,128)(2,1)} collective-permute-done((bf16[512,1408]{0,1:T(8,128)(2,1)}, bf16[512,1408]{0,1:T(8,128)(2,1)}, u32[]{:S(2)}, u32[]{:S(2)}) %collective-permute-start.1) | collective-permute-done | bytes 1441824 | tf_op jit(solution)/shard_map/ppermute | solution.py:14
  95.0 61.0 %all-gather.4.cloned.1.call-done = bf16[2816,2816]{1,0:T(8,128)(2,1)} async-done(((bf16[352,2816]{1,0:T(8,128)(2,1)}), bf16[2816,2816]{1,0:T(8,128)(2,1)}) %all-gather.4.cloned.1.call-update) | async-done | bytes 15859728 | tf_op jit(solution)/shard_map/all_gather | solution.py:55
  156.0 16.7 %fusion.114 = f32[512,2816]{1,0:T(8,128)} fusion(bf16[2816,2816]{1,0:T(8,128)(2,1)} %all-gather.4.cloned.1.call-done, bf16[512,1408]{0,1:T(8,128)(2,1)} %collective-permute-done.1, bf16[512,1408]{0,1:T(8,128)(2,1)} %maximum_select_fusion.1, pred[]{:T(512)S(6)} %eq.6), kind=kOutput, calls=%fused_computation.278 | convolution fusion | flops 8133148672 | bytes 24510464 | tf_op jit(solution)/shard_map/dot_general | solution.py:56
  172.7 126.8 %all-gather.6.cloned.1.call-done = bf16[2816,2816]{0,1:T(8,128)(2,1)} async-done(((bf16[2816,352]{0,1:T(8,128)(2,1)}), bf16[2816,2816]{0,1:T(8,128)(2,1)}) %all-gather.6.cloned.1.call-update) | async-done | bytes 15859728 | tf_op jit(solution)/shard_map/all_gather | solution.py:58
  299.5 16.3 %convolution_convert_fusion.3 = bf16[512,2816]{0,1:T(8,128)(2,1)} fusion(bf16[2816,2816]{0,1:T(8,128)(2,1)} %all-gather.6.cloned.1.call-done, f32[512,2816]{1,0:T(8,128)} %fusion.114), kind=kOutput, calls=%fused_computation.108 | convolution fusion | flops 8128823296 | bytes 24510464 | tf_op jit(solution)/shard_map/dot_general | solution.py:59
  315.8 0.0 all-gather.8.cloned.1.call-start
  315.8 2.5 copy.74
  318.3 1.6 copy.72
  319.9 36.0 %reduce-scatter.5.cloned.1.call-done = bf16[512,704]{0,1:T(8,128)(2,1)} async-done(((bf16[512,2816]{0,1:T(8,128)(2,1)}), bf16[512,704]{0,1:T(8,128)(2,1)}) %reduce-scatter.5.cloned.1.call-update) | async-done | bytes 720912 | tf_op jit(solution)/shard_map/reduce_scatter | solution.py:60
  355.9 3.5 fusion.109
  359.4 0.6 reduce-scatter.7.cloned.1.call-start
  360.0 41.4 %all-gather.8.cloned.1.call-done = bf16[512,2816]{0,1:T(8,128)(2,1)} async-done(((bf16[512,704]{0,1:T(8,128)(2,1)}), bf16[512,2816]{0,1:T(8,128)(2,1)}) %all-gather.8.cloned.1.call-update) | async-done | bytes 2883600 | tf_op jit(solution)/shard_map/all_gather | solution.py:68
  401.4 16.0 %fusion.5 = bf16[512,2816]{1,0:T(8,128)(2,1)S(1)} fusion(f32[512,2816]{1,0:T(8,128)} %fusion.114, bf16[512,2816]{0,1:T(8,128)(2,1)} %all-gather.8.cloned.1.call-done, bf16[2816,2816]{0,1:T(8,128)(2,1)} %all-gather.6.cloned.1.call-done), kind=kOutput, calls=%fused_computation.104 | convolution fusion | flops 8134590464 | bytes 27394048 | tf_op jit(solution)/shard_map/dot_general | solution.py:69
  417.4 1.6 copy-done.9
  419.0 13.0 %convolution_convert_fusion.2 = bf16[512,2816]{0,1:T(8,128)(2,1)} fusion(bf16[512,2816]{1,0:T(8,128)(2,1)S(1)} %fusion.5, bf16[2816,2816]{1,0:T(8,128)(2,1)} %all-gather.4.cloned.1.call-done), kind=kOutput, calls=%fused_computation.107 | convolution fusion | flops 8121614336 | bytes 21626880 | tf_op jit(solution)/shard_map/dot_general | solution.py:83
  432.1 0.0 all-reduce.6.cloned.1.call-start
  432.1 41.9 %reduce-scatter.7.cloned.1.call-done = bf16[512,704]{0,1:T(8,128)(2,1)} async-done(((bf16[512,2816]{0,1:T(8,128)(2,1)}), bf16[512,704]{0,1:T(8,128)(2,1)}) %reduce-scatter.7.cloned.1.call-update) | async-done | bytes 720912 | tf_op jit(solution)/shard_map/reduce_scatter | solution.py:86
  474.0 1.7 fusion.113
  475.7 9.1 %all-reduce.2 = (f32[512]{0:T(512)S(1)}, f32[512]{0:T(512)S(1)}) all-reduce(f32[512]{0:T(512)S(1)} %get-tuple-element.65, f32[512]{0:T(512)S(1)} %get-tuple-element.67), channel_id=1, replica_groups=mesh['dp'=8,'chan'=4] {'chan'}, use_global_device_ids=true, to_apply=%region_9.10 | all-reduce | flops 1024 | bytes 8192 | tf_op jit(solution)/shard_map/psum | solution.py:105
  484.8 2.6 fusion.111
  487.4 1.8 copy.75
  489.3 3.8 multiply_reduce_fusion.2
  493.1 4.2 multiply_reduce_fusion
  497.3 4.5 multiply_reduce_fusion.1
  502.9 0.6 copy-done.5
  503.5 0.0 reduce-scatter.11.cloned.1.call-start
  503.6 15.4 %convolution_convert_fusion = bf16[2816,2816]{1,0:T(8,128)(2,1)} fusion(bf16[512,2816]{0,1:T(8,128)(2,1)} %all-gather.8.cloned.1.call-done, f32[512,2816]{1,0:T(8,128)} %fusion.114), kind=kOutput, calls=%fused_computation.96 | convolution fusion | flops 8135311360 | bytes 24510464 | tf_op jit(solution)/shard_map/dot_general | solution.py:92
  519.0 0.3 reduce-scatter.9.cloned.1.call-start
  519.3 16.2 %convolution_convert_fusion.1 = bf16[2816,2816]{1,0:T(8,128)(2,1)} fusion(bf16[512,2816]{1,0:T(8,128)(2,1)} %copy-done.9, bf16[512,1408]{0,1:T(8,128)(2,1)} %collective-permute-done.1, bf16[512,1408]{0,1:T(8,128)(2,1)} %maximum_select_fusion.1, pred[]{:T(512)S(6)} %eq.6), kind=kOutput, calls=%fused_computation.97 | convolution fusion | flops 8141078528 | bytes 21626880 | tf_op jit(solution)/shard_map/dot_general | solution.py:76
  535.5 2.4 copy.73
  537.9 0.2 reduce_sum.567
  538.1 14.6 %all-reduce.3 = (bf16[704]{0:T(1024)(128)(2,1)S(1)}, bf16[704]{0:T(1024)(128)(2,1)S(1)}, bf16[704]{0:T(1024)(128)(2,1)S(1)}) all-reduce(bf16[704]{0:T(1024)(128)(2,1)S(1)} %get-tuple-element.64, bf16[704]{0:T(1024)(128)(2,1)S(1)} %reduce_sum.567, bf16[704]{0:T(1024)(128)(2,1)S(1)} %get-tuple-element.124), channel_id=1, replica_groups=mesh['dp'=8,'chan'=4] {'dp'}, use_global_device_ids=true, to_apply=%region_61.62 | all-reduce | flops 2112 | bytes 8448 | tf_op jit(solution)/shard_map/psum | solution.py:136
  552.7 0.6 convert_element_type.85
  553.3 0.6 convert_element_type.86
  553.9 0.6 convert_element_type.91
  554.5 12.3 %fusion.102 = bf16[2,16,16,704]{3,2,1,0:T(8,128)(2,1)} fusion(f32[2,16,16,704]{3,2,1,0:T(8,128)S(1)} %bitcast.80, f32[704]{0:T(1024)S(1)} %get-tuple-element.115, f32[704]{0:T(1024)S(1)} %get-tuple-element.116, f32[704]{0:T(1024)S(1)} %get-tuple-element.69, f32[704]{0:T(1024)S(1)} %get-tuple-element.70, f32[704]{0:T(1024)S(1)} %get-tuple-element.71, ...), kind=kLoop, calls=%fused_computation.211 | loop fusion | flops 36044800 | bytes 3021568 | tf_op jit(solution)/shard_map/convert_element_type | solution.py:133
  566.9 1.6 convert_element_type.83
  568.4 150.5 %reduce-scatter.11.cloned.1.call-done = bf16[352,2816]{1,0:T(8,128)(2,1)} async-done(((bf16[2816,2816]{1,0:T(8,128)(2,1)}), bf16[352,2816]{1,0:T(8,128)(2,1)}) %reduce-scatter.11.cloned.1.call-update) | async-done | bytes 1982480 | tf_op jit(solution)/shard_map/reduce_scatter | solution.py:91
  718.9 3.7 convert_bitcast_fusion
  722.6 156.7 %reduce-scatter.9.cloned.1.call-done = bf16[352,2816]{1,0:T(8,128)(2,1)} async-done(((bf16[2816,2816]{1,0:T(8,128)(2,1)}), bf16[352,2816]{1,0:T(8,128)(2,1)}) %reduce-scatter.9.cloned.1.call-update) | async-done | bytes 1982480 | tf_op jit(solution)/shard_map/reduce_scatter | solution.py:75
  879.4 3.7 convert_element_type.88
  (90 shorter events, 0.8 us)
Async XLA Ops:
  7.2 1.6 copy-start.2
  7.2 148.8 %all-gather.4.cloned.1.call-start = ((), (), s32[]{:S(2)}) async-start(), calls=%async_computation.4 | async-start | bytes 17842176 | tf_op jit(solution)/shard_map/all_gather | solution.py:55
  7.9 291.6 %all-gather.6.cloned.1.call-start = ((), (), s32[]{:S(2)}) async-start(), calls=%async_computation.5 | async-start | bytes 17842176 | tf_op jit(solution)/shard_map/all_gather | solution.py:58
  8.7 0.9 copy-start.4
  8.7 347.2 %reduce-scatter.5.cloned.1.call-start = ((), (), s32[]{:S(2)}) async-start(), calls=%async_computation.6 | async-start | bytes 3604480 | tf_op jit(solution)/shard_map/reduce_scatter | solution.py:60
  22.3 11.9 %copy-start = (f32[2,16,16,704]{3,2,1,0:T(8,128)}, f32[2,16,16,704]{3,2,1,0:T(8,128)S(1)}, u32[]{:S(2)}) copy-start(f32[2,16,16,704]{3,2,1,0:T(8,128)S(1)} %get-tuple-element.123) | copy-start | bytes 4325380
  34.2 10.3 %copy-start.6 = (f32[704]{0:T(1024)S(1)}, f32[704]{0:T(1024)}, u32[]{:S(2)}) copy-start(f32[704]{0:T(1024)} %param.10) | copy-start | bytes 8452
  34.2 10.2 %copy-start.7 = (f32[704]{0:T(1024)S(1)}, f32[704]{0:T(1024)}, u32[]{:S(2)}) copy-start(f32[704]{0:T(1024)} %param.11) | copy-start | bytes 8452
  45.6 15.8 %collective-permute-start = (bf16[512,704]{0,1:T(8,128)(2,1)}, bf16[512,704]{0,1:T(8,128)(2,1)}, u32[]{:S(2)}, u32[]{:S(2)}) collective-permute-start(bf16[512,704]{0,1:T(8,128)(2,1)} %add_convert_fusion), channel_id=1, source_target_pairs={{0,1},{1,0},{2,3},{3,2},{4,5},{5,4},{6,7},{7,6},{8,9},{9,8},{10,11... | collective-permute-start | bytes 2162696 | tf_op jit(solution)/shard_map/ppermute | solution.py:14
  64.7 30.3 %collective-permute-start.1 = (bf16[512,1408]{0,1:T(8,128)(2,1)}, bf16[512,1408]{0,1:T(8,128)(2,1)}, u32[]{:S(2)}, u32[]{:S(2)}) collective-permute-start(bf16[512,1408]{0,1:T(8,128)(2,1)} %maximum_select_fusion.1), channel_id=1, source_target_pairs={{0,2},{1,3},{2,0},{3,1},{4,6},{5,7},{6,4},{7,5},{8,10},{9,11},{10,... | collective-permute-start | bytes 4325384 | tf_op jit(solution)/shard_map/ppermute | solution.py:14
  315.8 85.6 %all-gather.8.cloned.1.call-start = ((), (), s32[]{:S(2)}) async-start(), calls=%async_computation.7 | async-start | bytes 3604480 | tf_op jit(solution)/shard_map/all_gather | solution.py:68
  318.3 37.6 %copy-start.8 = (f32[704]{0:T(1024)S(1)}, f32[704]{0:T(1024)}, u32[]{:S(2)}) copy-start(f32[704]{0:T(1024)} %param.14) | copy-start | bytes 8452
  359.4 114.6 %reduce-scatter.7.cloned.1.call-start = ((), (), s32[]{:S(2)}) async-start(), calls=%async_computation.8 | async-start | bytes 3604480 | tf_op jit(solution)/shard_map/reduce_scatter | solution.py:86
  417.4 1.6 copy-start.9
  432.1 134.8 %all-reduce.6.cloned.1.call-start = ((), (), s32[]{:S(2)}) async-start(), calls=%async_computation.9 | async-start | bytes 172032 | tf_op jit(solution)/shard_map/psum | solution.py:135
  502.9 0.6 copy-start.5
  503.5 215.4 %reduce-scatter.11.cloned.1.call-start = ((), (), s32[]{:S(2)}) async-start(), calls=%async_computation.11 | async-start | bytes 17842176 | tf_op jit(solution)/shard_map/reduce_scatter | solution.py:91
  519.0 360.4 %reduce-scatter.9.cloned.1.call-start = ((), (), s32[]{:S(2)}) async-start(), calls=%async_computation.10 | async-start | bytes 17842176 | tf_op jit(solution)/shard_map/reduce_scatter | solution.py:75
  535.5 2.4 copy-start.1
  535.5 19.0 %copy-start.3 = (bf16[2,16,16,704]{3,2,1,0:T(8,128)(2,1)S(1)}, bf16[2,16,16,704]{3,2,1,0:T(8,128)(2,1)}, u32[]{:S(2)}) copy-start(bf16[2,16,16,704]{3,2,1,0:T(8,128)(2,1)} %param.15) | copy-start | bytes 2162692
Sparse Core Ops, SparseCore 0:
  9.7 146.2 all-gather.3
  157.6 141.8 all-gather.5
  315.9 39.9 reduce-scatter.4
  359.5 41.7 all-gather.7
  432.2 41.7 reduce-scatter.6
  503.7 50.0 all-reduce.5
  556.2 162.6 reduce-scatter.10
  721.4 157.9 reduce-scatter.8
